TPU v7x, 32 devices: a whole 2x2x4 slice. The times are simulated.
32 devices in a mesh: dp: 8 (over z, x), mp: 4 (over y, core).
Axes of the slice: x: 2, y: 2, z: 4, core: 2. Of those that a mesh axis runs over, the one named last changes fastest.
Arguments:
- patches: bfloat16 [32000, 768], P(('dp', 'mp')), may hold values from -6 to 6
- dataset_id: int32 [160], P('dp'), may hold values from 0 to 7
- patch_masks: int32 [8, 200], replicated, may hold values 0 or 1
- mask_tokens: bfloat16 [8, 768], replicated, may hold values from -6 to 6
- key_mask: int32 [160, 200], P('dp'), may hold values from 0 to 1, as said below
- bias_index: int32 [200, 200], replicated, may hold values from 0 to 731
- norm1_gain: float32 [768], replicated, may hold values from 0.5 to 1.5
- norm1_shift: float32 [768], replicated, may hold values from -1.8 to 1.8
- qkv_weight: bfloat16 [768, 3, 768], P(None, None, 'mp'), may hold values from -0.21875 to 0.21875
- query_bias: bfloat16 [768], P('mp'), may hold values from -3 to 3
- value_bias: bfloat16 [768], P('mp'), may hold values from -3 to 3
- bias_table: bfloat16 [732, 12], P(None, 'mp'), may hold values from -5 to 5
- out_weight: bfloat16 [768, 768], P('mp'), may hold values from -1.75 to 1.75
- out_bias: float32 [768], replicated, may hold values from -1.8 to 1.8
- gamma_attn: float32 [768], replicated, may hold values from 0.5 to 2
- norm2_gain: float32 [768], replicated, may hold values from 0.5 to 1.5
- norm2_shift: float32 [768], replicated, may hold values from -1.8 to 1.8
- up_weight: bfloat16 [768, 3072], P(None, 'mp'), may hold values from -0.21875 to 0.21875
- up_bias: bfloat16 [3072], P('mp'), may hold values from -3 to 3
- down_weight: bfloat16 [3072, 768], P('mp'), may hold values from -0.109375 to 0.109375
- down_bias: float32 [768], replicated, may hold values from -1.8 to 1.8
- gamma_mlp: float32 [768], replicated, may hold values from 0.5 to 2
- cotangent: bfloat16 [32000, 768], P(('dp', 'mp')), may hold values from -6 to 6
Outputs:
- output: bfloat16 [32000, 768], P(('dp', 'mp'))
- patch_grad: float32 [32000, 768], P(('dp', 'mp'))
- token_grad: float32 [8, 768], replicated
- norm1_gain_grad: float32 [768], replicated
- norm1_shift_grad: float32 [768], replicated
- qkv_grad: float32 [768, 3, 768], P(None, None, 'mp')
- query_bias_grad: float32 [768], P('mp')
- value_bias_grad: float32 [768], P('mp')
- table_grad: float32 [732, 12], P(None, 'mp')
- out_weight_grad: float32 [768, 768], P('mp')
- out_bias_grad: float32 [768], replicated
- gamma_attn_grad: float32 [768], replicated
- norm2_gain_grad: float32 [768], replicated
- norm2_shift_grad: float32 [768], replicated
- up_weight_grad: float32 [768, 3072], P(None, 'mp')
- up_bias_grad: float32 [3072], P('mp')
- down_weight_grad: float32 [3072, 768], P('mp')
- down_bias_grad: float32 [768], replicated
- gamma_mlp_grad: float32 [768], replicated
Inputs may be any that keep to these rules, and one draw needn't show every extreme that they name: `key_mask`: each row holds ones on a prefix of its positions and zeros after it; the first position is always one.
All inputs are finite; a program needn't handle non-finite values.
Results may differ from a plain program's by a relative error of at most 0.013.
The roundings to bfloat16 on the way count: a program that leaves them out, or rounds other values in their place, can miss the bound.
Values may be sent and summed in bfloat16 or wider, within the bound.
No kernel may reach another device: no remote copies, remote signals or barrier semaphores. Data moves between devices by JAX's collectives and lax.ppermute only.
A program may use at most 192 MiB of HBM per device.

v0:
```python
import jax
import jax.numpy as jnp
from jax import lax
from jax.sharding import PartitionSpec as P

HEAD = 64
SEQ = 200
GROUPS = 8
IMG_BLK = 5


def layer_norm(values, gain, shift):
    mean = jnp.mean(values, axis=-1, keepdims=True)
    centred = values - mean
    spread = jnp.mean(centred * centred, axis=-1, keepdims=True)
    return centred * lax.rsqrt(spread + 1e-06) * gain + shift


def gelu_exact(values):
    return jax.nn.gelu(values, approximate=False)


def product(left, right):
    return jnp.dot(left, right, preferred_element_type=jnp.float32)


def product_first(left, right):
    return lax.dot_general(
        left, right, (((0,), (0,)), ((), ())), preferred_element_type=jnp.float32
    )


def product_last(left, right):
    return lax.dot_general(
        left, right, (((1,), (1,)), ((), ())), preferred_element_type=jnp.float32
    )


def product_cross(left, right):
    return lax.dot_general(
        left, right, (((0,), (1,)), ((), ())), preferred_element_type=jnp.float32
    )


def score_block(queries, keys, bias, key_mask):
    scores = (
        jnp.einsum("bqhe,bkhe->bhqk", queries, keys, preferred_element_type=jnp.float32)
        + bias[None]
    )
    return jnp.where(key_mask[:, None, None, :] > 0, scores, -1e30)


def attention_forward(normed, qkv_all, qbias_all, vbias_all, table_all, masks_here, position_table):
    width = qkv_all.shape[2]
    heads = width // HEAD
    images = masks_here.shape[0]
    scale = HEAD ** (-0.5)
    joint = product(normed, qkv_all.reshape(qkv_all.shape[0], 3 * width))
    shape5 = (images // IMG_BLK, IMG_BLK, SEQ, heads, HEAD)
    queries = (
        ((joint[:, :width] + qbias_all.astype(jnp.float32)) * scale)
        .astype(jnp.bfloat16)
        .reshape(shape5)
    )
    keys = joint[:, width : 2 * width].astype(jnp.bfloat16).reshape(shape5)
    values = (
        (joint[:, 2 * width :] + vbias_all.astype(jnp.float32)).astype(jnp.bfloat16).reshape(shape5)
    )
    bias_flat = product_cross(table_all, position_table)
    bias = bias_flat.reshape(heads, SEQ, SEQ)
    block_masks = masks_here.reshape(images // IMG_BLK, IMG_BLK, SEQ)

    def attend(pieces):
        block_q, block_k, block_v, block_mask = pieces
        scores = score_block(block_q, block_k, bias, block_mask)
        largest = jnp.max(scores, axis=-1, keepdims=True)
        lse = largest + jnp.log(jnp.sum(jnp.exp(scores - largest), axis=-1, keepdims=True))
        probs = jnp.exp(scores - lse).astype(jnp.bfloat16)
        context = jnp.einsum("bhqk,bkhe->bqhe", probs, block_v, preferred_element_type=jnp.float32)
        return (context.astype(jnp.bfloat16), lse)

    context, lse = lax.map(attend, (queries, keys, values, block_masks))
    return (queries, keys, values, block_masks, bias, context.reshape(images * SEQ, width), lse)


def attention_backward(queries, keys, values, block_masks, bias, lse, grad_context, position_table):
    heads = queries.shape[3]
    width = heads * HEAD
    scale = HEAD ** (-0.5)
    grad_blocks = grad_context.reshape(queries.shape)

    def step(total, pieces):
        block_q, block_k, block_v, block_mask, block_lse, block_grad = pieces
        scores = score_block(block_q, block_k, bias, block_mask)
        probs = jnp.exp(scores - block_lse)
        grad_probs = jnp.einsum(
            "bqhe,bkhe->bhqk", block_grad, block_v, preferred_element_type=jnp.float32
        )
        centre = jnp.sum(probs * grad_probs, axis=-1, keepdims=True)
        grad_scores = (probs * (grad_probs - centre)).astype(jnp.bfloat16)
        grad_values = jnp.einsum(
            "bhqk,bqhe->bkhe",
            probs.astype(jnp.bfloat16),
            block_grad,
            preferred_element_type=jnp.float32,
        ).astype(jnp.bfloat16)
        grad_queries = (
            jnp.einsum(
                "bhqk,bkhe->bqhe", grad_scores, block_k, preferred_element_type=jnp.float32
            ).astype(jnp.bfloat16)
            * scale
        )
        grad_keys = jnp.einsum(
            "bhqk,bqhe->bkhe", grad_scores, block_q, preferred_element_type=jnp.float32
        ).astype(jnp.bfloat16)
        total = total + jnp.sum(grad_scores.astype(jnp.float32), axis=0)
        return (total, (grad_queries, grad_keys, grad_values))

    start_total = jnp.zeros((heads, SEQ, SEQ), jnp.float32)
    total, (grad_q, grad_k, grad_v) = lax.scan(
        step, start_total, (queries, keys, values, block_masks, lse, grad_blocks)
    )
    rows = grad_context.shape[0]
    grad_q = grad_q.reshape(rows, width)
    grad_k = grad_k.reshape(rows, width)
    grad_v = grad_v.reshape(rows, width)
    grad_joint = jnp.concatenate([grad_q, grad_k, grad_v], axis=1)
    qbias_local = jnp.sum(grad_q.astype(jnp.float32), axis=0)
    vbias_local = jnp.sum(grad_v.astype(jnp.float32), axis=0)
    total_flat = total.reshape(heads, SEQ * SEQ)
    upper_part = total_flat.astype(jnp.bfloat16)
    lower_part = (total_flat - upper_part.astype(jnp.float32)).astype(jnp.bfloat16)
    stacked = jnp.concatenate([upper_part, lower_part], axis=0)
    table_both = product_cross(position_table, stacked)
    table_local = table_both[:, :heads] + table_both[:, heads:]
    return (grad_joint, qbias_local, vbias_local, table_local)


def local(
    patches,
    dataset_id,
    patch_masks,
    mask_tokens,
    key_mask,
    bias_index,
    norm1_gain,
    norm1_shift,
    qkv_weight,
    query_bias,
    value_bias,
    bias_table,
    out_weight,
    out_bias,
    gamma_attn,
    norm2_gain,
    norm2_shift,
    up_weight,
    up_bias,
    down_weight,
    down_bias,
    gamma_mlp,
    cotangent,
):
    rows = patches.shape[0]
    mp_count = lax.axis_size("mp")
    mp_place = lax.axis_index("mp")
    images = dataset_id.shape[0]
    own_images = images // mp_count
    table_rows = bias_table.shape[0]
    own_ids = lax.dynamic_slice_in_dim(dataset_id, mp_place * own_images, own_images, 0)
    own_choose = (own_ids[:, None] == jnp.arange(GROUPS)[None, :]).astype(jnp.bfloat16)
    own_sel = product(own_choose, patch_masks.astype(jnp.bfloat16))
    selected = own_sel.reshape(rows, 1)
    row_choose = jnp.broadcast_to(own_choose[:, None, :], (own_images, SEQ, GROUPS)).reshape(
        rows, GROUPS
    )
    token_rows = jnp.broadcast_to(
        product(own_choose, mask_tokens)[:, None, :], (own_images, SEQ, mask_tokens.shape[1])
    ).reshape(rows, mask_tokens.shape[1])
    position_table = (bias_index.reshape(SEQ * SEQ, 1) == jnp.arange(table_rows)[None, :]).astype(
        jnp.bfloat16
    )
    start = patches.astype(jnp.float32) * (1.0 - selected) + selected * token_rows
    norm1_value, norm1_back = jax.vjp(layer_norm, start, norm1_gain, norm1_shift)
    normed1 = norm1_value.astype(jnp.bfloat16)
    attn_in = lax.all_gather(normed1, "mp", axis=0, tiled=True)
    qkv_all, qbias_all, vbias_all, table_all, out_all = (
        qkv_weight,
        query_bias,
        value_bias,
        bias_table,
        out_weight,
    )
    queries, keys, values, block_masks, bias, context, lse = attention_forward(
        attn_in, qkv_all, qbias_all, vbias_all, table_all, key_mask, position_table
    )
    out_part = product(context, out_all)
    attn_sum = lax.psum_scatter(out_part, "mp", scatter_dimension=0, tiled=True)
    attn_value = attn_sum + out_bias
    middle = start + gamma_attn * attn_value
    norm2_value, norm2_back = jax.vjp(layer_norm, middle, norm2_gain, norm2_shift)
    normed2 = norm2_value.astype(jnp.bfloat16)
    mlp_in = lax.all_gather(normed2, "mp", axis=0, tiled=True)
    up_all, upb_all, down_all = (up_weight, up_bias, down_weight)
    hidden_pre = product(mlp_in, up_all) + upb_all.astype(jnp.float32)
    hidden_act, gelu_back = jax.vjp(gelu_exact, hidden_pre)
    hidden = hidden_act.astype(jnp.bfloat16)
    down_part = product(hidden, down_all)
    mlp_sum = lax.psum_scatter(
        down_part.astype(jnp.bfloat16), "mp", scatter_dimension=0, tiled=True
    ).astype(jnp.float32)
    mlp_value = mlp_sum + down_bias
    output = (middle + gamma_mlp * mlp_value).astype(jnp.bfloat16)
    grad_out = cotangent.astype(jnp.float32)
    gamma_mlp_part = jnp.sum(grad_out * mlp_value, axis=0)
    grad_mlp = (gamma_mlp * grad_out).astype(jnp.bfloat16)
    down_bias_part = jnp.sum(grad_mlp.astype(jnp.float32), axis=0)
    grad_mlp_all = lax.all_gather(grad_mlp, "mp", axis=0, tiled=True)
    down_grad_local = product_first(hidden, grad_mlp_all)
    grad_hidden = product_last(grad_mlp_all, down_all)
    grad_pre = gelu_back(grad_hidden)[0].astype(jnp.bfloat16)
    up_bias_local = jnp.sum(grad_pre.astype(jnp.float32), axis=0)
    up_grad_local = product_first(mlp_in, grad_pre)
    norm2_part = product_last(grad_pre, up_all)
    grad_normed2 = lax.psum_scatter(norm2_part, "mp", scatter_dimension=0, tiled=True)
    up_grad, up_bias_grad, down_grad = (up_grad_local, up_bias_local, down_grad_local)
    grad_middle_norm, norm2_gain_part, norm2_shift_part = norm2_back(grad_normed2)
    grad_middle = grad_out + grad_middle_norm
    gamma_attn_part = jnp.sum(grad_middle * attn_value, axis=0)
    grad_attn = (gamma_attn * grad_middle).astype(jnp.bfloat16)
    out_bias_part = jnp.sum(grad_attn.astype(jnp.float32), axis=0)
    grad_attn_all = lax.all_gather(grad_attn, "mp", axis=0, tiled=True)
    out_grad_local = product_first(context, grad_attn_all)
    grad_context = product_last(grad_attn_all, out_all).astype(jnp.bfloat16)
    grad_joint, qbias_local, vbias_local, table_local = attention_backward(
        queries, keys, values, block_masks, bias, lse, grad_context, position_table
    )
    width = qkv_all.shape[2]
    model_width = qkv_all.shape[0]
    qkv_grad_local = product_first(attn_in, grad_joint).reshape(model_width, 3, width)
    norm1_part = product_last(grad_joint, qkv_all.reshape(model_width, 3 * width))
    grad_normed1 = lax.psum_scatter(
        norm1_part.astype(jnp.bfloat16), "mp", scatter_dimension=0, tiled=True
    ).astype(jnp.float32)
    qkv_grad, qbias_grad, vbias_grad, table_grad, out_grad = (
        qkv_grad_local,
        qbias_local,
        vbias_local,
        table_local,
        out_grad_local,
    )
    grad_start_norm, norm1_gain_part, norm1_shift_part = norm1_back(grad_normed1)
    grad_start = grad_middle + grad_start_norm
    patch_grad = grad_start * (1.0 - selected)
    token_part = lax.dot_general(
        row_choose.astype(jnp.float32),
        grad_start * selected,
        (((0,), (0,)), ((), ())),
        precision=lax.Precision.HIGHEST,
    )
    qkv_grad, qbias_grad, vbias_grad, table_grad, out_grad, up_grad, up_bias_grad, down_grad = (
        lax.psum(
            (
                qkv_grad,
                qbias_grad,
                vbias_grad,
                table_grad,
                out_grad,
                up_grad,
                up_bias_grad,
                down_grad,
            ),
            "dp",
        )
    )
    (
        token_grad,
        norm1_gain_grad,
        norm1_shift_grad,
        out_bias_grad,
        gamma_attn_grad,
        norm2_gain_grad,
        norm2_shift_grad,
        down_bias_grad,
        gamma_mlp_grad,
    ) = lax.psum(
        (
            token_part,
            norm1_gain_part,
            norm1_shift_part,
            out_bias_part,
            gamma_attn_part,
            norm2_gain_part,
            norm2_shift_part,
            down_bias_part,
            gamma_mlp_part,
        ),
        ("dp", "mp"),
    )
    return (
        output,
        patch_grad,
        token_grad,
        norm1_gain_grad,
        norm1_shift_grad,
        qkv_grad,
        qbias_grad,
        vbias_grad,
        table_grad,
        out_grad,
        out_bias_grad,
        gamma_attn_grad,
        norm2_gain_grad,
        norm2_shift_grad,
        up_grad,
        up_bias_grad,
        down_grad,
        down_bias_grad,
        gamma_mlp_grad,
    )


def solution(mesh):
    return jax.shard_map(
        local,
        mesh=mesh,
        in_specs=(
            P(("dp", "mp"), None),
            P("dp"),
            P(),
            P(),
            P("dp", None),
            P(),
            P(),
            P(),
            P(None, None, "mp"),
            P("mp"),
            P("mp"),
            P(None, "mp"),
            P("mp", None),
            P(),
            P(),
            P(),
            P(),
            P(None, "mp"),
            P("mp"),
            P("mp", None),
            P(),
            P(),
            P(("dp", "mp"), None),
        ),
        out_specs=(
            P(("dp", "mp"), None),
            P(("dp", "mp"), None),
            P(),
            P(),
            P(),
            P(None, None, "mp"),
            P("mp"),
            P("mp"),
            P(None, "mp"),
            P("mp", None),
            P(),
            P(),
            P(),
            P(),
            P(None, "mp"),
            P("mp"),
            P("mp", None),
            P(),
            P(),
        ),
        check_vma=False,
    )
```

profile of v0, /device:TPU:0, one launch (start us, length us, event | category | flops | bytes accessed | tf_op | source)
XLA Modules:
  0.0 1081.7 jit_solution(13086309809975984235)
XLA Ops:
  18.2 3.9 add_convert_fusion.3
  22.6 18.9 %fusion.61 = f32[3,40000]{1,0:T(4,128)} fusion(bf16[732,3]{0,1:T(4,128)(2,1)S(1)} %copy-done.62, s32[40000]{0:T(1024)S(1)} %eq.35), kind=kOutput, calls=%fused_computation.71 | convolution fusion | flops 204960000 | bytes 644392 | tf_op jit(solution)/shard_map/dot_general | solution.py:40
  44.3 26.1 %all-gather.5.cloned.1.call-done = bf16[4000,768]{1,0:T(8,128)(2,1)} async-done(((bf16[1000,768]{1,0:T(8,128)(2,1)}), bf16[4000,768]{1,0:T(8,128)(2,1)}) %all-gather.5.cloned.1.call-update) | async-done | bytes 6144016 | tf_op jit(solution)/shard_map/all_gather | solution.py:186
  70.5 6.2 fusion.95
  80.6 7.3 reshape.237
  87.9 4.5 copy.113
  92.3 7.6 reshape.239
  100.0 4.5 copy.114
  104.5 7.3 reshape.240
  111.7 4.5 copy.115
  117.7 30.9 %while.31 = (s32[]{:T(128)}, bf16[4,5,200,3,64]{2,4,3,1,0:T(8,128)(2,1)}, f32[4,5,3,200,1]{3,2,1,4,0:T(4,128)}, bf16[4,5,200,3,64]{2,4,3,1,0:T(8,128)(2,1)}, s32...) while((s32[]{:T(128)}, ...), condition=%wide.wide.region_5.6_spmd, body=%wide.wide.region_2.5_spmd.sunk | while | flops 160390000 | bytes 11681225 | solution.py:82
  148.5 4.5 copy.116
  153.0 5.7 reshape.241
  158.8 7.7 fusion.96
  166.7 97.1 %reduce-scatter.5.cloned.1.call-done = f32[1000,768]{1,0:T(8,128)} async-done(((f32[4000,768]{1,0:T(8,128)}), f32[1000,768]{1,0:T(8,128)}) %reduce-scatter.5.cloned.1.call-update) | async-done | bytes 3072016 | tf_op jit(solution)/shard_map/reduce_scatter | solution.py:198
  263.8 4.3 multiply_add_fusion
  277.0 43.4 %all-gather.7.cloned.1.call-done = bf16[4000,768]{1,0:T(8,128)(2,1)} async-done(((bf16[1000,768]{1,0:T(8,128)(2,1)}), bf16[4000,768]{1,0:T(8,128)(2,1)}) %all-gather.7.cloned.1.call-update) | async-done | bytes 6144016 | tf_op jit(solution)/shard_map/all_gather | solution.py:203
  320.4 13.8 %fusion.97 = f32[4000,768]{1,0:T(8,128)} fusion(bf16[4000,768]{1,0:T(8,128)(2,1)} %all-gather.7.cloned.1.call-done, bf16[768,768]{1,0:T(8,128)(2,1)} %param.44), kind=kOutput, calls=%fused_computation.165 | convolution fusion | flops 4718592000 | bytes 19611648 | tf_op jit(solution)/shard_map/dot_general | solution.py:24
  334.2 33.8 %all-gather.9.cloned.1.call-done = bf16[4000,768]{1,0:T(8,128)(2,1)} async-done(((bf16[1000,768]{1,0:T(8,128)(2,1)}), bf16[4000,768]{1,0:T(8,128)(2,1)}) %all-gather.9.cloned.1.call-update) | async-done | bytes 6144016 | tf_op jit(solution)/shard_map/all_gather | solution.py:218
  368.0 36.0 %convert_reduce_fusion.1 = (f32[768]{0:T(1024)}, bf16[4000,768]{1,0:T(8,128)(2,1)S(1)}, f32[4000,768]{1,0:T(8,128)}) fusion(f32[4000,768]{1,0:T(8,128)} %fusion.97, f32[768]{0:T(1024)S(1)} %convert_element_type.138, bf16[4000,768]{1,0:T(8,128)(2,1)} %all-gather.9.cloned.1.call-done, bf16[768,768]{1,0:T(8,128)(2,1)S(1)} %copy-done), kind=kOutput, calls=%fused_computation.74 | convolution fusion | flops 4948990976 | bytes 38049792 | tf_op jit(solution)/shard_map/dot_general | solution.py:34
  406.5 7.9 fusion.98
  414.7 11.1 %multiply_convert_fusion.1 = bf16[4000,768]{1,0:T(8,128)(2,1)S(1)} fusion(f32[4000,768]{1,0:T(8,128)} %get-tuple-element.343, f32[4000,768]{1,0:T(8,128)} %fusion.97, f32[768]{0:T(1024)S(1)} %convert_element_type.138), kind=kLoop, calls=%fused_computation.76 | loop fusion | flops 12288000 | bytes 30723072 | tf_op jit(solution)/shard_map/convert_element_type | solution.py:207
  425.8 3.7 copy-done.21
  429.5 6.8 convolution_convert_fusion.3
  436.4 75.3 %reduce-scatter.9.cloned.1.call-done = f32[1000,768]{1,0:T(8,128)} async-done(((f32[4000,768]{1,0:T(8,128)}), f32[1000,768]{1,0:T(8,128)}) %reduce-scatter.9.cloned.1.call-update) | async-done | bytes 3072016 | tf_op jit(solution)/shard_map/reduce_scatter | solution.py:225
  514.6 56.9 %reduce-scatter.7.cloned.1.call-done = bf16[1000,768]{1,0:T(8,128)(2,1)} async-done(((bf16[4000,768]{1,0:T(8,128)(2,1)}), bf16[1000,768]{1,0:T(8,128)(2,1)}) %reduce-scatter.7.cloned.1.call-update) | async-done | bytes 1536016 | tf_op jit(solution)/shard_map/reduce_scatter | solution.py:209
  571.6 4.3 fusion.94
  580.2 43.9 %all-gather.11.cloned.1.call-done = bf16[4000,768]{1,0:T(8,128)(2,1)} async-done(((bf16[1000,768]{1,0:T(8,128)(2,1)}), bf16[4000,768]{1,0:T(8,128)(2,1)}) %all-gather.11.cloned.1.call-update) | async-done | bytes 6144016 | tf_op jit(solution)/shard_map/all_gather | solution.py:232
  624.1 6.0 convolution_convert_fusion.4
  630.1 6.7 reshape.242
  644.0 85.4 %while.32 = (s32[]{:T(128)}, f32[3,200,200]{1,2,0:T(8,128)}, bf16[4,5,200,3,64]{2,4,3,1,0:T(8,128)(2,1)}, bf16[4,5,200,3,64]{2,4,3,1,0:T(8,128)(2,1)}, bf16[4,5,...) while((s32[]{:T(128)}, f32[3,200,200]{1,2,0:T(8,128)}, ...), condition=%wide.wide.region_16.17_spmd.clone, body=%wide.wide.region_13.16_spmd.clone.sunk | while | flops 392062016 | bytes 36752904 | solution.py:120
  651.1 3.6 multiply_reduce_fusion.8
  672.3 3.6 multiply_reduce_fusion.8
  732.3 4.0 reshape.243
  742.1 5.1 reshape.244
  750.2 4.8 reshape.245
  757.6 9.4 convolution_convert_fusion.2
  767.7 10.0 fusion.100
  777.7 10.6 fusion.101
  789.2 5.1 fusion.99
  794.4 7.8 fusion.102
  806.3 23.4 %fusion.57 = f32[732,6]{0,1:T(8,128)S(1)} fusion(s32[40000]{0:T(1024)} %copy-done.36, bf16[3,40000]{1,0:T(4,128)(2,1)S(1)} %get-tuple-element.344, bf16[3,40000]{1,0:T(4,128)(2,1)} %get-tuple-element.345), kind=kOutput, calls=%fused_computation.67 | convolution fusion | flops 381600000 | bytes 657568 | tf_op jit(solution)/shard_map/dot_general | solution.py:40
  829.8 39.7 %all-reduce.1 = (f32[192]{0:T(256)}, f32[192]{0:T(256)}, f32[732,3]{0,1:T(4,128)}, f32[768]{0:T(1024)}) all-reduce(f32[192]{0:T(256)S(1)} %reduce_sum.245, f32[192]{0:T(256)S(1)} %reduce_sum.247, f32[732,3]{0,1:T(4,128)S(1)} %slice_add_fusion.2, f32[768]{0:T(1024)S(1)} %copy-done.55), channel_id=1, replica_groups=mesh['dp'=8,'mp'=4] {'dp'}, use_global_device_ids=true, to_apply=%region_27.28 | all-reduce | flops 3348 | bytes 26784 | tf_op jit(solution)/shard_map/psum | solution.py:262
  869.6 4.1 fusion.76
  879.4 4.4 fusion.77
  884.3 4.1 fusion.75
  888.4 41.2 %all-reduce = (f32[8,768]{1,0:T(8,128)}, f32[768]{0:T(1024)}, f32[768]{0:T(1024)}, f32[768]{0:T(1024)}, f32[768]{0:T(1024)}, /*index=5*/f32[768]{0:T(1024)}, f32[768]{0:T(1024)}, f32[768]{0:T(1024)}, f32[768]{0:T(1024)}) all-reduce(f32[8,768]{1,0:T(8,128)S(1)} %fusion.77, ...), channel_id=1, replica_groups=mesh['dp'=8,'mp'=4] {'dp','mp'}, use_global_device_ids=true, to_apply=%region_20.21 | all-reduce | flops 12288 | bytes 98304 | tf_op jit(solution)/shard_map/psum | solution.py:286
  929.6 138.8 %all-reduce.5.cloned.1.call-done = (f32[768,3,192]{0,2,1:T(8,128)}, f32[192,768]{1,0:T(8,128)}, f32[768,768]{1,0:T(8,128)}, f32[768,768]{1,0:T(8,128)}) async-done(((f32[768,3,192]{0,2,1:T(8,128)}, f32[192,768]{1,0:T(8,128)}, f32[768,768]{1,0:T(8,128)}, f32[768,768]{1,0:T(8,128)}), (f32[768,3,192]{0,2,1:T(8,128)}, f32[192,768]{1,0:T(8,128)}, f32[768,768]{1,0:T(8,128)}, ...) | async-done | bytes 7077904 | tf_op jit(solution)/shard_map/psum | solution.py:262
  (282 shorter events, 187.4 us)
Async XLA Ops:
  7.2 360.8 %copy-start = (bf16[768,768]{1,0:T(8,128)(2,1)S(1)}, bf16[768,768]{1,0:T(8,128)(2,1)}, u32[]{:S(2)}) copy-start(bf16[768,768]{1,0:T(8,128)(2,1)} %param.46) | copy-start | bytes 3538948
  7.2 63.3 %all-gather.5.cloned.1.call-start = ((), (), s32[]{:S(2)}) async-start(), calls=%async_computation.4 | async-start | bytes 7680000 | tf_op jit(solution)/shard_map/all_gather | solution.py:186
  8.1 5.4 copy-start.58
  9.0 254.7 %copy-start.31 = (f32[1000]{0:T(1024)}, f32[1000]{0:T(1024)S(1)}, u32[]{:S(2)}) copy-start(f32[1000]{0:T(1024)S(1)} %reshape.234) | copy-start | bytes 12004
  9.0 254.7 %copy-start.34 = (f32[1000]{0:T(1024)}, f32[1000]{0:T(1024)S(1)}, u32[]{:S(2)}) copy-start(f32[1000]{0:T(1024)S(1)} %broadcast_subtract_fusion) | copy-start | bytes 12004
  10.0 253.8 %copy-start.25 = (f32[5,768]{1,0:T(8,128)}, f32[5,768]{1,0:T(8,128)S(1)}, u32[]{:S(2)}) copy-start(f32[5,768]{1,0:T(8,128)S(1)} %fusion.86) | copy-start | bytes 46084
  13.5 4.7 copy-start.9
  13.5 4.7 copy-start.42
  13.5 4.7 copy-start.54
  15.7 6.3 copy-start.37
  18.1 23.5 %copy-start.44 = (f32[1000]{0:T(1024)}, f32[1000]{0:T(1024)S(1)}, u32[]{:S(2)}) copy-start(f32[1000]{0:T(1024)S(1)} %multiply_reduce_fusion.5) | copy-start | bytes 12004
  18.1 4.5 copy-start.62
  18.2 23.4 %copy-start.39 = (f32[1000]{0:T(1024)}, f32[1000]{0:T(1024)S(1)}, u32[]{:S(2)}) copy-start(f32[1000]{0:T(1024)S(1)} %fusion.87) | copy-start | bytes 12004
  22.1 241.7 %reduce-scatter.5.cloned.1.call-start = ((), (), s32[]{:S(2)}) async-start(), calls=%async_computation.5 | async-start | bytes 15360000 | tf_op jit(solution)/shard_map/reduce_scatter | solution.py:198
  22.6 18.9 %copy-start.36 = (s32[40000]{0:T(1024)}, s32[40000]{0:T(1024)S(1)}, u32[]{:S(2)}) copy-start(s32[40000]{0:T(1024)S(1)} %eq.35) | copy-start | bytes 480004
  22.6 21.7 %copy-start.46 = (s32[20,200]{1,0:T(8,128)S(1)}, s32[20,200]{1,0:T(8,128)}, u32[]{:S(2)}) copy-start(s32[20,200]{1,0:T(8,128)} %param.31) | copy-start | bytes 48004
  148.5 10.2 copy-start.28
  153.0 5.7 copy-start.29
  166.4 97.3 %copy-start.48 = (f32[768]{0:T(1024)S(1)}, f32[768]{0:T(1024)}, u32[]{:S(2)}) copy-start(f32[768]{0:T(1024)} %param.40) | copy-start | bytes 9220
  166.4 97.3 %copy-start.51 = (f32[768]{0:T(1024)S(1)}, f32[768]{0:T(1024)}, u32[]{:S(2)}) copy-start(f32[768]{0:T(1024)} %param.41) | copy-start | bytes 9220
  166.5 153.9 %all-gather.7.cloned.1.call-start = ((), (), s32[]{:S(2)}) async-start(), calls=%async_computation.6 | async-start | bytes 7680000 | tf_op jit(solution)/shard_map/all_gather | solution.py:203
  268.1 4.6 copy-start.41
  268.1 4.7 copy-start.56
  274.7 93.3 %all-gather.9.cloned.1.call-start = ((), (), s32[]{:S(2)}) async-start(), calls=%async_computation.8 | async-start | bytes 7680000 | tf_op jit(solution)/shard_map/all_gather | solution.py:218
  276.9 234.8 %reduce-scatter.9.cloned.1.call-start = ((), (), s32[]{:S(2)}) async-start(), calls=%async_computation.9 | async-start | bytes 15360000 | tf_op jit(solution)/shard_map/reduce_scatter | solution.py:225
  334.2 72.3 %copy-start.60 = (bf16[768,768]{1,0:T(8,128)(2,1)S(1)}, bf16[768,768]{1,0:T(8,128)(2,1)}, u32[]{:S(2)}) copy-start(bf16[768,768]{1,0:T(8,128)(2,1)} %param.44) | copy-start | bytes 3538948
  414.5 157.1 %reduce-scatter.7.cloned.1.call-start = ((), (), s32[]{:S(2)}) async-start(), calls=%async_computation.7 | async-start | bytes 7680000 | tf_op jit(solution)/shard_map/reduce_scatter | solution.py:209
  436.3 75.4 %copy-start.4 = (f32[1000,768]{1,0:T(8,128)S(1)}, f32[1000,768]{1,0:T(8,128)}, u32[]{:S(2)}) copy-start(f32[1000,768]{1,0:T(8,128)} %multiply_add_fusion) | copy-start | bytes 9216004
  436.3 135.2 %copy-start.50 = (f32[768]{0:T(1024)S(1)}, f32[768]{0:T(1024)}, u32[]{:S(2)}) copy-start(f32[768]{0:T(1024)} %param.47) | copy-start | bytes 9220
  436.3 187.7 %all-gather.11.cloned.1.call-start = ((), (), s32[]{:S(2)}) async-start(), calls=%async_computation.10 | async-start | bytes 7680000 | tf_op jit(solution)/shard_map/all_gather | solution.py:232
  575.9 48.1 %copy-start.30 = (bf16[192,768]{1,0:T(8,128)(2,1)S(1)}, bf16[192,768]{1,0:T(8,128)(2,1)}, u32[]{:S(2)}) copy-start(bf16[192,768]{1,0:T(8,128)(2,1)} %param.39) | copy-start | bytes 884740
  578.4 291.1 %reduce-scatter.11.cloned.1.call-start = ((), (), s32[]{:S(2)}) async-start(), calls=%async_computation.11 | async-start | bytes 7680000 | tf_op jit(solution)/shard_map/reduce_scatter | solution.py:242
  742.1 5.1 copy-start.16
  767.0 301.4 %all-reduce.5.cloned.1.call-start = ((), (), s32[]{:S(2)}) async-start(), calls=%async_computation.12 | async-start | bytes 14155776 | tf_op jit(solution)/shard_map/psum | solution.py:262
  777.7 10.6 copy-start.14
  777.7 11.5 %copy-start.19 = (bf16[4000,192]{0,1:T(8,128)(2,1)S(1)}, bf16[4000,192]{0,1:T(8,128)(2,1)}, u32[]{:S(2)}) copy-start(bf16[4000,192]{0,1:T(8,128)(2,1)} %reshape.241) | copy-start | bytes 4608004
  788.6 5.8 slice-start
  789.2 5.2 slice-start.1
  806.3 23.5 %copy-start.55 = (f32[768]{0:T(1024)S(1)}, f32[768]{0:T(1024)}, u32[]{:S(2)}) copy-start(f32[768]{0:T(1024)} %get-tuple-element.341) | copy-start | bytes 9220
  806.3 63.2 %copy-start.5 = (f32[1000,768]{1,0:T(8,128)S(1)}, f32[1000,768]{1,0:T(8,128)}, u32[]{:S(2)}) copy-start(f32[1000,768]{1,0:T(8,128)} %multiply_add_fusion.1) | copy-start | bytes 9216004
  806.3 63.2 %copy-start.26 = (f32[5,768]{1,0:T(8,128)S(1)}, f32[5,768]{1,0:T(8,128)}, u32[]{:S(2)}) copy-start(f32[5,768]{1,0:T(8,128)} %copy-done.25) | copy-start | bytes 46084
  806.3 63.2 %copy-start.32 = (f32[1000]{0:T(1024)S(1)}, f32[1000]{0:T(1024)}, u32[]{:S(2)}) copy-start(f32[1000]{0:T(1024)} %copy-done.31) | copy-start | bytes 12004
  806.3 63.2 %copy-start.35 = (f32[1000]{0:T(1024)S(1)}, f32[1000]{0:T(1024)}, u32[]{:S(2)}) copy-start(f32[1000]{0:T(1024)} %copy-done.34) | copy-start | bytes 12004
  806.3 63.2 %copy-start.38 = (f32[1000]{0:T(1024)S(1)}, f32[1000]{0:T(1024)}, u32[]{:S(2)}) copy-start(f32[1000]{0:T(1024)} %copy-done.37) | copy-start | bytes 12004
  806.3 63.2 %copy-start.40 = (f32[1000]{0:T(1024)S(1)}, f32[1000]{0:T(1024)}, u32[]{:S(2)}) copy-start(f32[1000]{0:T(1024)} %copy-done.39) | copy-start | bytes 12004
  806.3 63.2 %copy-start.43 = (f32[768]{0:T(1024)S(1)}, f32[768]{0:T(1024)}, u32[]{:S(2)}) copy-start(f32[768]{0:T(1024)} %param.33) | copy-start | bytes 9220
  879.4 4.9 copy-start.17
  879.4 4.9 copy-start.49
  (32 other events, 103.5 us)
Sparse Core Ops, SparseCore 0:
  22.2 48.2 all-gather.4
  166.6 97.1 reduce-scatter.4
  274.8 45.5 all-gather.6
  322.4 45.5 all-gather.8
  414.6 97.0 reduce-scatter.8
  514.1 57.3 reduce-scatter.6
  578.5 45.5 all-gather.10
  767.1 57.3 reduce-scatter.10
  830.7 237.6 all-reduce.4
where the time goes:
time: 1090 us; the launch traced here: 1080 us
  waiting for transfers between devices  515 us (47%)
  matrix products  252 us (23%)
  local copies, waits for them, and re-layouts  130 us (12%)
  other arithmetic  87.4 us (8%)
  blocking collectives  80.9 us (7%)
  between operations  14.8 us (1%)
    psum x1, waiting for transfers between devices, local(): lax.psum((qkv_grad, qbias_grad, vbias_grad, table_grad, out_grad, up_grad...  139 us
    reduce_scatter x1, waiting for transfers between devices, local(): attn_sum = lax.psum_scatter(out_part, 'mp', scatter_dimension=0, tiled=True)  97.1 us
    reduce_scatter x1, waiting for transfers between devices, local(): lax.psum_scatter(norm2_part, 'mp', scatter_dimension=0, tiled=True)  75.3 us
    dot_general x4, matrix products, product_last(): lax.dot_general(left, right, (((1,), (1,)), ((), ())), preferred_element_...  59.3 us
    reduce_scatter x1, waiting for transfers between devices, local(): lax.psum_scatter(down_part.astype(jnp.bfloat16), 'mp', scatter_dimension=...  56.9 us
    all_gather x1, waiting for transfers between devices, local(): grad_attn_all = lax.all_gather(grad_attn, 'mp', axis=0, tiled=True)  43.9 us
    all_gather x1, waiting for transfers between devices, local(): mlp_in = lax.all_gather(normed2, 'mp', axis=0, tiled=True)  43.4 us
    dot_general x2, matrix products, product_cross(): lax.dot_general(left, right, (((0,), (1,)), ((), ())), preferred_element_...  42.3 us
  transfers between devices with their start and end apart: 9, of which 8 were waited for; matrix products, arithmetic and copies ran while one was open for 13% of the time, Pallas kernels for 0%

commit v1 on v0

--- a/solution.py
+++ b/solution.py
@@ -7,6 +7,17 @@
 SEQ = 200
 GROUPS = 8
 IMG_BLK = 5
+
+
+def gather_around(array, axis, dim):
+    ways = lax.axis_size(axis)
+    pieces = [array]
+    for far in range(1, ways):
+        pieces.append(
+            lax.ppermute(pieces[far - 1], axis, [(d, (d - 1) % ways) for d in range(ways)])
+        )
+    line = jnp.concatenate(pieces, axis=dim)
+    return jnp.roll(line, lax.axis_index(axis) * array.shape[dim], axis=dim)
 
 
 def layer_norm(values, gain, shift):
@@ -183,7 +194,7 @@
     start = patches.astype(jnp.float32) * (1.0 - selected) + selected * token_rows
     norm1_value, norm1_back = jax.vjp(layer_norm, start, norm1_gain, norm1_shift)
     normed1 = norm1_value.astype(jnp.bfloat16)
-    attn_in = lax.all_gather(normed1, "mp", axis=0, tiled=True)
+    attn_in = gather_around(normed1, "mp", 0)
     qkv_all, qbias_all, vbias_all, table_all, out_all = (
         qkv_weight,
         query_bias,

time: 1090 us -> 1120 us (1.028)
  local copies, waits for them, and re-layouts: 130 us -> 147 us
    ppermute x0 -> x3, waiting for transfers between devices: none -> 35.1 us  [gather_around(): lax.ppermute(pieces[far - 1], axis, [(d, (d - 1) % ways) for d in range(w...]
    all_gather x1 -> x0, waiting for transfers between devices: 26.1 us -> none  [local(): attn_in = lax.all_gather(normed1, 'mp', axis=0, tiled=True)]
    unnamed x141 -> x157, local copies, waits for them, and re-layouts: 22.3 us -> 37 us
  transfers between devices with their start and end apart: 9 -> 11, of which waited for: 8 -> 9; matrix products, arithmetic and copies ran while one was open for 13% -> 13% of each run, Pallas kernels for 0% -> 0%
where the time goes in v1:
time: 1120 us; the launch traced here: 1110 us
  waiting for transfers between devices  525 us (47%)
  matrix products  252 us (22%)
  local copies, waits for them, and re-layouts  147 us (13%)
  other arithmetic  85.6 us (8%)
  blocking collectives  81.1 us (7%)
  between operations  15.1 us (1%)
    psum x1, waiting for transfers between devices, local(): lax.psum((qkv_grad, qbias_grad, vbias_grad, table_grad, out_grad, up_grad...  139 us
    reduce_scatter x1, waiting for transfers between devices, local(): attn_sum = lax.psum_scatter(out_part, 'mp', scatter_dimension=0, tiled=True)  97.5 us
    reduce_scatter x1, waiting for transfers between devices, local(): lax.psum_scatter(norm2_part, 'mp', scatter_dimension=0, tiled=True)  75.6 us
    dot_general x4, matrix products, product_last(): lax.dot_general(left, right, (((1,), (1,)), ((), ())), preferred_element_...  59.4 us
    reduce_scatter x1, waiting for transfers between devices, local(): lax.psum_scatter(down_part.astype(jnp.bfloat16), 'mp', scatter_dimension=...  56.9 us
    all_gather x1, waiting for transfers between devices, local(): grad_attn_all = lax.all_gather(grad_attn, 'mp', axis=0, tiled=True)  43.5 us
    all_gather x1, waiting for transfers between devices, local(): mlp_in = lax.all_gather(normed2, 'mp', axis=0, tiled=True)  43.5 us
    dot_general x2, matrix products, product_cross(): lax.dot_general(left, right, (((0,), (1,)), ((), ())), preferred_element_...  42.3 us
  transfers between devices with their start and end apart: 11, of which 9 were waited for; matrix products, arithmetic and copies ran while one was open for 13% of the time, Pallas kernels for 0%

profile of v1, /device:TPU:0, one launch (start us, length us, event | category | flops | bytes accessed | tf_op | source)
XLA Modules:
  0.0 1113.0 jit_solution(13149396859731735882)
XLA Ops:
  22.7 17.5 %collective-permute-done = bf16[1000,768]{1,0:T(8,128)(2,1)S(1)} collective-permute-done((bf16[1000,768]{1,0:T(8,128)(2,1)S(1)}, bf16[1000,768]{1,0:T(8,128)(2,1)S(1)}, u32[]{:S(2)}, u32[]{:S(2)}) %collective-permute-start) | collective-permute-done | bytes 1536032 | tf_op jit(solution)/shard_map/ppermute | solution.py:17
  43.3 17.5 %collective-permute-done.1 = bf16[1000,768]{1,0:T(8,128)(2,1)} collective-permute-done((bf16[1000,768]{1,0:T(8,128)(2,1)S(1)}, bf16[1000,768]{1,0:T(8,128)(2,1)}, u32[]{:S(2)}, u32[]{:S(2)}) %collective-permute-start.1) | collective-permute-done | bytes 1536032 | tf_op jit(solution)/shard_map/ppermute | solution.py:17
  63.3 18.9 %fusion.61 = f32[3,40000]{1,0:T(4,128)} fusion(bf16[732,3]{0,1:T(4,128)(2,1)S(1)} %copy-done.67, s32[40000]{0:T(1024)S(1)} %eq.38), kind=kOutput, calls=%fused_computation.71 | convolution fusion | flops 204960000 | bytes 644392 | tf_op jit(solution)/shard_map/dot_general | solution.py:51
  101.2 6.0 fusion.70
  111.1 7.4 reshape.237
  118.6 4.5 copy.113
  123.1 7.2 reshape.239
  130.3 4.5 copy.114
  134.8 7.2 reshape.240
  142.0 4.6 copy.115
  148.1 30.9 %while.31 = (s32[]{:T(128)}, bf16[4,5,200,3,64]{2,4,3,1,0:T(8,128)(2,1)}, f32[4,5,3,200,1]{3,2,1,4,0:T(4,128)}, bf16[4,5,200,3,64]{2,4,3,1,0:T(8,128)(2,1)}, s32...) while((s32[]{:T(128)}, ...), condition=%wide.wide.region_5.6_spmd, body=%wide.wide.region_2.5_spmd.sunk | while | flops 160390000 | bytes 11681225 | solution.py:93
  179.0 4.5 copy.116
  183.5 6.1 reshape.241
  189.6 7.6 fusion.101
  197.3 97.5 %reduce-scatter.5.cloned.1.call-done = f32[1000,768]{1,0:T(8,128)} async-done(((f32[4000,768]{1,0:T(8,128)}), f32[1000,768]{1,0:T(8,128)}) %reduce-scatter.5.cloned.1.call-update) | async-done | bytes 3072016 | tf_op jit(solution)/shard_map/reduce_scatter | solution.py:209
  294.9 4.3 multiply_add_fusion
  308.1 43.5 %all-gather.4.cloned.1.call-done = bf16[4000,768]{1,0:T(8,128)(2,1)} async-done(((bf16[1000,768]{1,0:T(8,128)(2,1)}), bf16[4000,768]{1,0:T(8,128)(2,1)}) %all-gather.4.cloned.1.call-update) | async-done | bytes 6144016 | tf_op jit(solution)/shard_map/all_gather | solution.py:214
  351.5 13.9 %fusion.102 = f32[4000,768]{1,0:T(8,128)} fusion(bf16[4000,768]{1,0:T(8,128)(2,1)} %all-gather.4.cloned.1.call-done, bf16[768,768]{1,0:T(8,128)(2,1)} %param.44), kind=kOutput, calls=%fused_computation.178 | convolution fusion | flops 4718592000 | bytes 19611648 | tf_op jit(solution)/shard_map/dot_general | solution.py:35
  365.4 33.9 %all-gather.6.cloned.1.call-done = bf16[4000,768]{1,0:T(8,128)(2,1)} async-done(((bf16[1000,768]{1,0:T(8,128)(2,1)}), bf16[4000,768]{1,0:T(8,128)(2,1)}) %all-gather.6.cloned.1.call-update) | async-done | bytes 6144016 | tf_op jit(solution)/shard_map/all_gather | solution.py:229
  399.2 36.1 %convert_reduce_fusion.1 = (f32[768]{0:T(1024)}, bf16[4000,768]{1,0:T(8,128)(2,1)S(1)}, f32[4000,768]{1,0:T(8,128)}) fusion(f32[4000,768]{1,0:T(8,128)} %fusion.102, f32[768]{0:T(1024)S(1)} %convert_element_type.138, bf16[4000,768]{1,0:T(8,128)(2,1)} %all-gather.6.cloned.1.call-done, bf16[768,768]{1,0:T(8,128)(2,1)S(1)} %copy-done), kind=kOutput, calls=%fused_computation.74 | convolution fusion | flops 4948990976 | bytes 38049792 | tf_op jit(solution)/shard_map/dot_general | solution.py:45
  437.9 7.9 fusion.103
  445.9 10.9 multiply_convert_fusion.1
  456.8 3.8 copy-done.25
  460.6 6.9 convolution_convert_fusion.3
  467.5 75.6 %reduce-scatter.9.cloned.1.call-done = f32[1000,768]{1,0:T(8,128)} async-done(((f32[4000,768]{1,0:T(8,128)}), f32[1000,768]{1,0:T(8,128)}) %reduce-scatter.9.cloned.1.call-update) | async-done | bytes 3072016 | tf_op jit(solution)/shard_map/reduce_scatter | solution.py:236
  546.0 56.9 %reduce-scatter.7.cloned.1.call-done = bf16[1000,768]{1,0:T(8,128)(2,1)} async-done(((bf16[4000,768]{1,0:T(8,128)(2,1)}), bf16[1000,768]{1,0:T(8,128)(2,1)}) %reduce-scatter.7.cloned.1.call-update) | async-done | bytes 1536016 | tf_op jit(solution)/shard_map/reduce_scatter | solution.py:220
  602.9 4.3 fusion.100
  611.9 43.5 %all-gather.8.cloned.1.call-done = bf16[4000,768]{1,0:T(8,128)(2,1)} async-done(((bf16[1000,768]{1,0:T(8,128)(2,1)}), bf16[4000,768]{1,0:T(8,128)(2,1)}) %all-gather.8.cloned.1.call-update) | async-done | bytes 6144016 | tf_op jit(solution)/shard_map/all_gather | solution.py:243
  655.4 6.0 convolution_convert_fusion.4
  661.5 6.4 reshape.242
  674.9 85.6 %while.32 = (s32[]{:T(128)}, f32[3,200,200]{1,2,0:T(8,128)}, bf16[4,5,200,3,64]{2,4,3,1,0:T(8,128)(2,1)}, bf16[4,5,200,3,64]{2,4,3,1,0:T(8,128)(2,1)}, bf16[4,5,...) while((s32[]{:T(128)}, f32[3,200,200]{1,2,0:T(8,128)}, ...), condition=%wide.wide.region_16.17_spmd.clone, body=%wide.wide.region_13.16_spmd.clone.sunk | while | flops 392062016 | bytes 36752904 | solution.py:131
  682.0 3.6 multiply_reduce_fusion.8
  703.2 3.6 multiply_reduce_fusion.8
  763.4 4.0 reshape.243
  773.2 5.1 reshape.244
  781.3 4.8 reshape.245
  788.6 9.3 convolution_convert_fusion.2
  798.6 10.0 fusion.105
  808.6 10.6 fusion.106
  820.2 5.1 fusion.104
  825.3 7.8 fusion.68
  837.3 23.4 %fusion.57 = f32[732,6]{0,1:T(8,128)S(1)} fusion(s32[40000]{0:T(1024)} %copy-done.40, bf16[3,40000]{1,0:T(4,128)(2,1)S(1)} %get-tuple-element.344, bf16[3,40000]{1,0:T(4,128)(2,1)} %get-tuple-element.345), kind=kOutput, calls=%fused_computation.67 | convolution fusion | flops 381600000 | bytes 657568 | tf_op jit(solution)/shard_map/dot_general | solution.py:51
  860.7 39.9 %all-reduce.1 = (f32[192]{0:T(256)}, f32[192]{0:T(256)}, f32[732,3]{0,1:T(4,128)}, f32[768]{0:T(1024)}) all-reduce(f32[192]{0:T(256)S(1)} %reduce_sum.245, f32[192]{0:T(256)S(1)} %reduce_sum.247, f32[732,3]{0,1:T(4,128)S(1)} %slice_add_fusion.2, f32[768]{0:T(1024)S(1)} %copy-done.58), channel_id=1, replica_groups=mesh['dp'=8,'mp'=4] {'dp'}, use_global_device_ids=true, to_apply=%region_27.28 | all-reduce | flops 3348 | bytes 26784 | tf_op jit(solution)/shard_map/psum | solution.py:273
  900.7 4.1 fusion.80
  910.4 4.4 fusion.81
  915.3 4.1 fusion.79
  919.4 41.2 %all-reduce = (f32[8,768]{1,0:T(8,128)}, f32[768]{0:T(1024)}, f32[768]{0:T(1024)}, f32[768]{0:T(1024)}, f32[768]{0:T(1024)}, /*index=5*/f32[768]{0:T(1024)}, f32[768]{0:T(1024)}, f32[768]{0:T(1024)}, f32[768]{0:T(1024)}) all-reduce(f32[8,768]{1,0:T(8,128)S(1)} %fusion.81, ...), channel_id=1, replica_groups=mesh['dp'=8,'mp'=4] {'dp','mp'}, use_global_device_ids=true, to_apply=%region_20.21 | all-reduce | flops 12288 | bytes 98304 | tf_op jit(solution)/shard_map/psum | solution.py:297
  960.6 138.7 %all-reduce.5.cloned.1.call-done = (f32[768,3,192]{0,2,1:T(8,128)}, f32[192,768]{1,0:T(8,128)}, f32[768,768]{1,0:T(8,128)}, f32[768,768]{1,0:T(8,128)}) async-done(((f32[768,3,192]{0,2,1:T(8,128)}, f32[192,768]{1,0:T(8,128)}, f32[768,768]{1,0:T(8,128)}, f32[768,768]{1,0:T(8,128)}), (f32[768,3,192]{0,2,1:T(8,128)}, f32[192,768]{1,0:T(8,128)}, f32[768,768]{1,0:T(8,128)}, ...) | async-done | bytes 7077904 | tf_op jit(solution)/shard_map/psum | solution.py:273
  (302 shorter events, 213.0 us)
Async XLA Ops:
  7.2 392.0 %copy-start = (bf16[768,768]{1,0:T(8,128)(2,1)S(1)}, bf16[768,768]{1,0:T(8,128)(2,1)}, u32[]{:S(2)}) copy-start(bf16[768,768]{1,0:T(8,128)(2,1)} %param.46) | copy-start | bytes 3538948
  7.2 287.6 %reduce-scatter.5.cloned.1.call-start = ((), (), s32[]{:S(2)}) async-start(), calls=%async_computation.4 | async-start | bytes 15360000 | tf_op jit(solution)/shard_map/reduce_scatter | solution.py:209
  8.1 5.4 copy-start.62
  9.0 285.8 %copy-start.35 = (f32[1000]{0:T(1024)}, f32[1000]{0:T(1024)S(1)}, u32[]{:S(2)}) copy-start(f32[1000]{0:T(1024)S(1)} %reshape.234) | copy-start | bytes 12004
  9.0 285.8 %copy-start.38 = (f32[1000]{0:T(1024)}, f32[1000]{0:T(1024)S(1)}, u32[]{:S(2)}) copy-start(f32[1000]{0:T(1024)S(1)} %broadcast_subtract_fusion) | copy-start | bytes 12004
  10.0 284.9 %copy-start.29 = (f32[5,768]{1,0:T(8,128)}, f32[5,768]{1,0:T(8,128)S(1)}, u32[]{:S(2)}) copy-start(f32[5,768]{1,0:T(8,128)S(1)} %fusion.90) | copy-start | bytes 46084
  18.1 64.2 %copy-start.46 = (f32[1000]{0:T(1024)}, f32[1000]{0:T(1024)S(1)}, u32[]{:S(2)}) copy-start(f32[1000]{0:T(1024)S(1)} %multiply_reduce_fusion.5) | copy-start | bytes 12004
  18.1 45.0 %copy-start.68 = (bf16[192]{0:T(256)(128)(2,1)S(1)}, bf16[192]{0:T(256)(128)(2,1)}, u32[]{:S(2)}) copy-start(bf16[192]{0:T(256)(128)(2,1)} %param.37) | copy-start | bytes 1156
  18.1 44.9 %copy-start.69 = (bf16[192]{0:T(256)(128)(2,1)S(1)}, bf16[192]{0:T(256)(128)(2,1)}, u32[]{:S(2)}) copy-start(bf16[192]{0:T(256)(128)(2,1)} %param.36) | copy-start | bytes 1156
  18.1 44.9 %copy-start.37 = (s32[200,200]{1,0:T(8,128)S(1)}, s32[200,200]{1,0:T(8,128)}, u32[]{:S(2)}) copy-start(s32[200,200]{1,0:T(8,128)} %param.32) | copy-start | bytes 480004
  18.1 45.2 %copy-start.67 = (bf16[732,3]{0,1:T(4,128)(2,1)S(1)}, bf16[732,3]{0,1:T(4,128)(2,1)}, u32[]{:S(2)}) copy-start(bf16[732,3]{0,1:T(4,128)(2,1)} %param.38) | copy-start | bytes 13180
  18.2 64.1 %copy-start.43 = (f32[1000]{0:T(1024)}, f32[1000]{0:T(1024)S(1)}, u32[]{:S(2)}) copy-start(f32[1000]{0:T(1024)S(1)} %fusion.91) | copy-start | bytes 12004
  20.3 40.5 %copy-start.23 = (bf16[1000,768]{1,0:T(8,128)(2,1)}, bf16[1000,768]{1,0:T(8,128)(2,1)S(1)}, u32[]{:S(2)}) copy-start(bf16[1000,768]{1,0:T(8,128)(2,1)S(1)} %get-tuple-element.361) | copy-start | bytes 4608004
  20.3 19.9 %collective-permute-start = (bf16[1000,768]{1,0:T(8,128)(2,1)S(1)}, bf16[1000,768]{1,0:T(8,128)(2,1)S(1)}, u32[]{:S(2)}, u32[]{:S(2)}) collective-permute-start(bf16[1000,768]{1,0:T(8,128)(2,1)S(1)} %get-tuple-element.361), channel_id=1, source_target_pairs={{0,3},{1,0},{2,1},{3,2},{4,7},{5,4},{6,5},{7,6},{8,11},{9,8},{10,9... | collective-permute-start | bytes 4608008 | tf_op jit(solution)/shard_map/ppermute | solution.py:17
  41.4 19.4 %collective-permute-start.1 = (bf16[1000,768]{1,0:T(8,128)(2,1)S(1)}, bf16[1000,768]{1,0:T(8,128)(2,1)}, u32[]{:S(2)}, u32[]{:S(2)}) collective-permute-start(bf16[1000,768]{1,0:T(8,128)(2,1)S(1)} %collective-permute-done), channel_id=1, source_target_pairs={{0,3},{1,0},{2,1},{3,2},{4,7},{5,4},{6,5},{7,6},{8,11},{9,8},{10,9... | collective-permute-start | bytes 4608008 | tf_op jit(solution)/shard_map/ppermute | solution.py:17
  60.8 29.6 %collective-permute-start.2 = (bf16[1000,768]{1,0:T(8,128)(2,1)}, bf16[1000,768]{1,0:T(8,128)(2,1)}, u32[]{:S(2)}, u32[]{:S(2)}) collective-permute-start(bf16[1000,768]{1,0:T(8,128)(2,1)} %collective-permute-done.1), channel_id=1, source_target_pairs={{0,3},{1,0},{2,1},{3,2},{4,7},{5,4},{6,5},{7,6},{8,11},{9,8},{10,9... | collective-permute-start | bytes 4608008 | tf_op jit(solution)/shard_map/ppermute | solution.py:17
  63.3 18.9 %copy-start.40 = (s32[40000]{0:T(1024)}, s32[40000]{0:T(1024)S(1)}, u32[]{:S(2)}) copy-start(s32[40000]{0:T(1024)S(1)} %eq.38) | copy-start | bytes 480004
  63.3 21.7 %copy-start.50 = (s32[20,200]{1,0:T(8,128)S(1)}, s32[20,200]{1,0:T(8,128)}, u32[]{:S(2)}) copy-start(s32[20,200]{1,0:T(8,128)} %param.31) | copy-start | bytes 48004
  87.7 5.6 copy-start.24
  95.8 5.3 copy-start.65
  179.0 10.6 copy-start.32
  183.5 6.1 copy-start.33
  197.2 97.6 %copy-start.52 = (f32[768]{0:T(1024)S(1)}, f32[768]{0:T(1024)}, u32[]{:S(2)}) copy-start(f32[768]{0:T(1024)} %param.40) | copy-start | bytes 9220
  197.2 97.6 %copy-start.55 = (f32[768]{0:T(1024)S(1)}, f32[768]{0:T(1024)}, u32[]{:S(2)}) copy-start(f32[768]{0:T(1024)} %param.41) | copy-start | bytes 9220
  197.3 154.2 %all-gather.4.cloned.1.call-start = ((), (), s32[]{:S(2)}) async-start(), calls=%async_computation.5 | async-start | bytes 7680000 | tf_op jit(solution)/shard_map/all_gather | solution.py:214
  305.8 93.4 %all-gather.6.cloned.1.call-start = ((), (), s32[]{:S(2)}) async-start(), calls=%async_computation.7 | async-start | bytes 7680000 | tf_op jit(solution)/shard_map/all_gather | solution.py:229
  308.0 235.1 %reduce-scatter.9.cloned.1.call-start = ((), (), s32[]{:S(2)}) async-start(), calls=%async_computation.8 | async-start | bytes 15360000 | tf_op jit(solution)/shard_map/reduce_scatter | solution.py:236
  365.4 72.6 %copy-start.64 = (bf16[768,768]{1,0:T(8,128)(2,1)S(1)}, bf16[768,768]{1,0:T(8,128)(2,1)}, u32[]{:S(2)}) copy-start(bf16[768,768]{1,0:T(8,128)(2,1)} %param.44) | copy-start | bytes 3538948
  445.8 157.1 %reduce-scatter.7.cloned.1.call-start = ((), (), s32[]{:S(2)}) async-start(), calls=%async_computation.6 | async-start | bytes 7680000 | tf_op jit(solution)/shard_map/reduce_scatter | solution.py:220
  467.4 75.7 %copy-start.4 = (f32[1000,768]{1,0:T(8,128)S(1)}, f32[1000,768]{1,0:T(8,128)}, u32[]{:S(2)}) copy-start(f32[1000,768]{1,0:T(8,128)} %multiply_add_fusion) | copy-start | bytes 9216004
  467.5 135.5 %copy-start.54 = (f32[768]{0:T(1024)S(1)}, f32[768]{0:T(1024)}, u32[]{:S(2)}) copy-start(f32[768]{0:T(1024)} %param.47) | copy-start | bytes 9220
  467.5 187.9 %all-gather.8.cloned.1.call-start = ((), (), s32[]{:S(2)}) async-start(), calls=%async_computation.9 | async-start | bytes 7680000 | tf_op jit(solution)/shard_map/all_gather | solution.py:243
  607.3 48.1 %copy-start.34 = (bf16[192,768]{1,0:T(8,128)(2,1)S(1)}, bf16[192,768]{1,0:T(8,128)(2,1)}, u32[]{:S(2)}) copy-start(bf16[192,768]{1,0:T(8,128)(2,1)} %param.39) | copy-start | bytes 884740
  609.7 290.9 %reduce-scatter.11.cloned.1.call-start = ((), (), s32[]{:S(2)}) async-start(), calls=%async_computation.10 | async-start | bytes 7680000 | tf_op jit(solution)/shard_map/reduce_scatter | solution.py:253
  773.2 5.1 copy-start.16
  797.9 301.4 %all-reduce.5.cloned.1.call-start = ((), (), s32[]{:S(2)}) async-start(), calls=%async_computation.11 | async-start | bytes 14155776 | tf_op jit(solution)/shard_map/psum | solution.py:273
  808.6 10.6 copy-start.14
  808.6 11.5 %copy-start.19 = (bf16[4000,192]{0,1:T(8,128)(2,1)S(1)}, bf16[4000,192]{0,1:T(8,128)(2,1)}, u32[]{:S(2)}) copy-start(bf16[4000,192]{0,1:T(8,128)(2,1)} %reshape.241) | copy-start | bytes 4608004
  819.5 5.8 slice-start
  820.2 5.2 slice-start.1
  837.2 23.5 %copy-start.58 = (f32[768]{0:T(1024)S(1)}, f32[768]{0:T(1024)}, u32[]{:S(2)}) copy-start(f32[768]{0:T(1024)} %get-tuple-element.341) | copy-start | bytes 9220
  837.2 63.4 %copy-start.5 = (f32[1000,768]{1,0:T(8,128)S(1)}, f32[1000,768]{1,0:T(8,128)}, u32[]{:S(2)}) copy-start(f32[1000,768]{1,0:T(8,128)} %multiply_add_fusion.1) | copy-start | bytes 9216004
  837.2 63.4 %copy-start.30 = (f32[5,768]{1,0:T(8,128)S(1)}, f32[5,768]{1,0:T(8,128)}, u32[]{:S(2)}) copy-start(f32[5,768]{1,0:T(8,128)} %copy-done.29) | copy-start | bytes 46084
  837.2 63.4 %copy-start.36 = (f32[1000]{0:T(1024)S(1)}, f32[1000]{0:T(1024)}, u32[]{:S(2)}) copy-start(f32[1000]{0:T(1024)} %copy-done.35) | copy-start | bytes 12004
  837.2 63.4 %copy-start.39 = (f32[1000]{0:T(1024)S(1)}, f32[1000]{0:T(1024)}, u32[]{:S(2)}) copy-start(f32[1000]{0:T(1024)} %copy-done.38) | copy-start | bytes 12004
  837.2 63.4 %copy-start.42 = (f32[1000]{0:T(1024)S(1)}, f32[1000]{0:T(1024)}, u32[]{:S(2)}) copy-start(f32[1000]{0:T(1024)} %copy-done.41) | copy-start | bytes 12004
  837.2 63.4 %copy-start.44 = (f32[1000]{0:T(1024)S(1)}, f32[1000]{0:T(1024)}, u32[]{:S(2)}) copy-start(f32[1000]{0:T(1024)} %copy-done.43) | copy-start | bytes 12004
  837.3 63.4 %copy-start.49 = (f32[768]{0:T(1024)S(1)}, f32[768]{0:T(1024)}, u32[]{:S(2)}) copy-start(f32[768]{0:T(1024)} %param.33) | copy-start | bytes 9220
  (39 other events, 133.6 us)
Sparse Core Ops, SparseCore 0:
  197.4 97.3 reduce-scatter.4
  305.9 45.5 all-gather.3
  353.6 45.5 all-gather.5
  445.9 97.1 reduce-scatter.8
  545.5 57.3 reduce-scatter.6
  609.8 45.5 all-gather.7
  798.0 57.3 reduce-scatter.10
  861.6 237.6 all-reduce.4
